TPU v7x, 256 devices: a whole 4x4x8 slice. The times are simulated.
256 devices in a mesh: trial: 8 (over y_hi, x), dp: 8 (over z), tensor: 4 (over y_lo, core).
Axes of the slice: x: 4, y: 4 (y_hi: 2, y_lo: 2; y = y_hi * 2 + y_lo), z: 8, core: 2. Of those that a mesh axis runs over, the one named last changes fastest.
Arguments:
- residual_rows: bfloat16 [32768, 8192], P(('trial', 'dp', 'tensor'))
- input_norm_weight: float32 [8192], replicated, may hold values from 0.25 to 1.75
- trial_row_index: int32 [8, 4096], P(None, 'dp'), may hold values from 0 to 127, as said below
- keyvalue_weight: bfloat16 [8192, 2048], P('tensor'), may hold values from -0.0625 to 0.0625
- adapter_down_weight: bfloat16 [8, 8192, 128], P('trial', 'tensor'), may hold values from -0.0625 to 0.0625
- adapter_up_weight: bfloat16 [8, 64, 2048], P('trial'), may hold values from -0.75 to 0.75
- keyvalue_gradient: bfloat16 [8, 4096, 2048], P('trial', ('dp', 'tensor')), may hold values from -6 to 6
Outputs:
- keyvalue_output: float32 [8, 4096, 2048], P('trial', ('dp', 'tensor'))
- grad_a: float32 [8, 128, 8192], P('trial', 'dp', 'tensor')
- grad_b: float32 [8, 64, 2048], P('trial', None, ('dp', 'tensor'))
Inputs may be any that keep to these rules, and one draw needn't show every extreme that they name: `trial_row_index`: within each trial, each index of dp and each block of 16 consecutive tokens taken from one source device, the rows named are distinct.
All inputs are finite; a program needn't handle non-finite values.
Results may differ from a plain program's by a relative error of at most 0.0041.
Values may be sent and summed in bfloat16 or wider, within the bound.
A program may use at most 64 MiB of HBM per device.

v0:
```python
import jax
import jax.numpy as jnp
from jax import lax
from jax.sharding import PartitionSpec as P

adapter_scale = 2.0
norm_eps = 1e-05


def shards(
    residual_rows,
    input_norm_weight,
    trial_row_index,
    keyvalue_weight,
    adapter_down_weight,
    adapter_up_weight,
    keyvalue_gradient,
):
    trials = lax.axis_size("trial")
    tensors = lax.axis_size("tensor")
    dps = lax.axis_size("dp")
    tok_dev = trial_row_index.shape[1]
    select = tok_dev // (trials * tensors)
    normed_input = keyvalue_weight.shape[0]
    kv_width = keyvalue_weight.shape[1]
    keyvalue_half = kv_width // 2
    rank_index = adapter_up_weight.shape[1]
    pool_dev = residual_rows.shape[0]
    highest_precision = lax.Precision.HIGHEST
    source = lax.axis_index("trial") * tensors + lax.axis_index("tensor")
    picks = lax.dynamic_slice_in_dim(trial_row_index, source * select, select, 1).reshape(-1)
    onehot = (picks[:, None] == jnp.arange(pool_dev, dtype=jnp.int32)[None, :]).astype(jnp.bfloat16)
    wide = jnp.dot(onehot, residual_rows, preferred_element_type=jnp.float32)
    msq = jnp.mean(wide * wide, axis=1, keepdims=True)
    chosen = (wide * lax.rsqrt(msq + norm_eps) * input_norm_weight[None, :]).astype(jnp.bfloat16)
    chosen = chosen.reshape(trials, select, tensors, normed_input).transpose(0, 2, 1, 3)
    arrived = lax.all_to_all(
        chosen.reshape(trials * tensors, select, normed_input),
        ("trial", "tensor"),
        split_axis=0,
        concat_axis=0,
        tiled=True,
    )
    rows = arrived.reshape(tok_dev, normed_input)
    up_weight = adapter_up_weight[0].astype(jnp.float32)
    grad_in = keyvalue_gradient[0].astype(jnp.float32)
    key_gradient_full = jnp.dot(
        grad_in[:, :keyvalue_half], up_weight[:, :keyvalue_half].T, precision=highest_precision
    )
    value_gradient_full = jnp.dot(
        grad_in[:, keyvalue_half:], up_weight[:, keyvalue_half:].T, precision=highest_precision
    )
    rank_gradient = (
        adapter_scale * jnp.concatenate([key_gradient_full, value_gradient_full], axis=1)
    ).astype(jnp.bfloat16)
    every_rank = lax.all_gather(rank_gradient, "tensor", axis=0, tiled=True)
    grad_a_term = lax.dot_general(
        every_rank, rows, (((0,), (0,)), ((), ())), preferred_element_type=jnp.float32
    )
    down_weight = adapter_down_weight[0]
    keyval = jnp.dot(rows, keyvalue_weight, preferred_element_type=jnp.float32)
    ranks = jnp.dot(rows, down_weight, preferred_element_type=jnp.float32)
    summed = lax.psum_scatter(
        jnp.concatenate([keyval, ranks], axis=1), "tensor", scatter_dimension=0, tiled=True
    )
    frozen_output_local = summed[:, :kv_width]
    local_rank_rows = summed[:, kv_width:]
    adapter_key = jnp.dot(
        local_rank_rows[:, :rank_index], up_weight[:, :keyvalue_half], precision=highest_precision
    )
    adapter_value = jnp.dot(
        local_rank_rows[:, rank_index:], up_weight[:, keyvalue_half:], precision=highest_precision
    )
    keyvalue_output = frozen_output_local + adapter_scale * jnp.concatenate(
        [adapter_key, adapter_value], axis=1
    )
    grad_a = lax.psum_scatter(grad_a_term, "dp", scatter_dimension=0, tiled=True)
    key_down_gradient = jnp.dot(
        local_rank_rows[:, :rank_index].T, grad_in[:, :keyvalue_half], precision=highest_precision
    )
    value_down_gradient = jnp.dot(
        local_rank_rows[:, rank_index:].T, grad_in[:, keyvalue_half:], precision=highest_precision
    )
    up_gradient_term = adapter_scale * jnp.concatenate(
        [key_down_gradient, value_down_gradient], axis=1
    )
    width = up_gradient_term.shape[1] // (dps * tensors)
    up_gradient_term = (
        up_gradient_term.reshape(rank_index, dps, tensors, width)
        .transpose(0, 2, 1, 3)
        .reshape(rank_index, dps * tensors * width)
    )
    grad_b = lax.psum_scatter(up_gradient_term, "tensor", scatter_dimension=1, tiled=True)
    grad_b = lax.psum_scatter(grad_b, "dp", scatter_dimension=1, tiled=True)
    return (keyvalue_output[None], grad_a[None], grad_b[None])


def solution(mesh):
    return jax.shard_map(
        shards,
        mesh=mesh,
        in_specs=(
            P(("trial", "dp", "tensor"), None),
            P(),
            P(None, "dp"),
            P("tensor", None),
            P("trial", "tensor", None),
            P("trial", None, None),
            P("trial", ("dp", "tensor"), None),
        ),
        out_specs=(
            P("trial", ("dp", "tensor"), None),
            P("trial", "dp", "tensor"),
            P("trial", None, ("dp", "tensor")),
        ),
        check_vma=False,
    )
```

profile of v0, /device:TPU:4, one launch (start us, length us, event | category | flops | bytes accessed | tf_op | source)
XLA Modules:
  0.0 229.4 jit_solution(2438023686047598556)
XLA Ops:
  7.2 0.9 constant_dynamic-slice_fusion
  8.1 0.1 eq.15
  8.2 0.6 copy-done
  8.8 0.8 multiply_reduce_fusion
  9.6 1.8 multiply_convert_fusion
  11.5 4.5 %reshape.31 = bf16[8,16,4,2048]{3,2,1,0:T(4,128)(2,1)} reshape(bf16[128,8192]{1,0:T(8,128)(2,1)} %multiply_convert_fusion) | data formatting | bytes 4194304 | tf_op jit(solution)/shard_map/reshape | solution.py:36
  16.0 2.8 %copy.15 = bf16[8,16,4,2048]{3,1,2,0:T(8,128)(2,1)S(1)} copy(bf16[8,16,4,2048]{3,2,1,0:T(4,128)(2,1)} %reshape.31) | data formatting | bytes 4194304 | tf_op jit(solution)/shard_map/reshape | solution.py:36
  18.8 34.8 %all_to_all.5 = bf16[32,16,2048]{2,1,0:T(8,128)(2,1)S(1)} all-to-all(bf16[32,16,2048]{2,1,0:T(8,128)(2,1)S(1)} %bitcast.28), channel_id=1, replica_groups=mesh['trial'=8,'dp'=8,'tensor'=4] {'trial','tensor'}, dimensions={0} | all-to-all | bytes 4194304 | tf_op jit(solution)/shard_map/all_to_all | solution.py:37
  53.6 0.7 fusion.2
  54.3 0.6 copy-done.1
  54.9 6.9 %fusion.25 = f32[512,2048]{1,0:T(8,128)S(1)} fusion(bf16[512,2048]{1,0:T(8,128)(2,1)S(1)} %bitcast.26, bf16[2048,2048]{1,0:T(8,128)(2,1)} %param.10), kind=kOutput, calls=%fused_computation.35 | convolution fusion | flops 4294967296 | bytes 14680064 | tf_op jit(solution)/shard_map/dot_general | solution.py:61
  61.8 2.4 %pad_maximum_fusion = f32[512,2176]{1,0:T(8,128)} fusion(f32[512,128]{1,0:T(8,128)S(1)} %fusion.2, f32[512,2048]{1,0:T(8,128)S(1)} %fusion.25), kind=kLoop, calls=%fused_computation | loop fusion | flops 1114112 | bytes 8912896 | tf_op jit(solution)/shard_map/concatenate | solution.py:64
  64.3 51.0 %reduce-scatter.7.cloned.1.call-done = f32[128,2176]{1,0:T(8,128)} async-done(((f32[512,2176]{1,0:T(8,128)}), f32[128,2176]{1,0:T(8,128)}) %reduce-scatter.7.cloned.1.call-update) | async-done | bytes 1114128 | tf_op jit(solution)/shard_map/reduce_scatter | solution.py:63
  115.3 1.2 fusion.8
  116.5 0.3 concatenate.20
  116.8 1.4 fusion.4
  118.2 0.3 concatenate.21
  118.6 0.3 fusion.1
  118.9 0.1 copy.17
  119.0 1.2 reshape.34
  120.2 1.2 fusion.10
  121.4 1.2 fusion.6
  122.6 5.4 %all_gather.3 = bf16[512,128]{0,1:T(8,128)(2,1)S(1)} all-gather(bf16[128,128]{0,1:T(8,128)(2,1)S(1)} %fusion.18), channel_id=1, replica_groups=mesh['trial'=8,'dp'=8,'tensor'=4] {'tensor'}, dimensions={0}, use_global_device_ids=true | all-gather | bytes 163840 | tf_op jit(solution)/shard_map/all_gather | solution.py:56
  128.0 14.0 %reduce-scatter.11.cloned.1.call-done = f32[64,512]{1,0:T(8,128)} async-done(((f32[64,2048]{1,0:T(8,128)}), f32[64,512]{1,0:T(8,128)}) %reduce-scatter.11.cloned.1.call-update) | async-done | bytes 131088 | tf_op jit(solution)/shard_map/reduce_scatter | solution.py:93
  142.0 1.7 copy.19
  143.8 3.1 %fusion.26 = f32[128,2048]{1,0:T(8,128)} fusion(bf16[512,128]{0,1:T(8,128)(2,1)S(1)} %all_gather.3, bf16[512,2048]{1,0:T(8,128)(2,1)} %bitcast.27), kind=kOutput, calls=%fused_computation.36 | convolution fusion | flops 268435456 | bytes 3276800 | tf_op jit(solution)/shard_map/dot_general | solution.py:57
  146.9 1.3 fusion.13
  148.3 1.3 fusion.16
  149.5 1.1 fusion
  150.7 31.6 %reduce-scatter.13.cloned.1.call-done = f32[64,64]{1,0:T(8,128)} async-done(((f32[512,64]{1,0:T(8,128)}), f32[64,64]{1,0:T(8,128)}) %reduce-scatter.13.cloned.1.call-update) | async-done | bytes 16400
  182.3 1.5 copy.20
  183.8 39.1 %reduce-scatter.9.cloned.1.call-done = f32[16,2048]{1,0:T(8,128)} async-done(((f32[128,2048]{1,0:T(8,128)}), f32[16,2048]{1,0:T(8,128)}) %reduce-scatter.9.cloned.1.call-update) | async-done | bytes 131088 | tf_op jit(solution)/shard_map/reduce_scatter | solution.py:77
  (22 shorter events, 0.3 us)
Async XLA Ops:
  7.2 1.6 copy-start
  7.2 108.1 %reduce-scatter.7.cloned.1.call-start = ((), (), s32[]{:S(2)}) async-start(), calls=%async_computation.5 | async-start | bytes 5570560 | tf_op jit(solution)/shard_map/reduce_scatter | solution.py:63
  8.8 0.8 copy-start.6
  18.7 34.8 %copy-start.4 = (bf16[1,2048,128]{2,1,0:T(8,128)(2,1)S(1)}, bf16[1,2048,128]{2,1,0:T(8,128)(2,1)}, u32[]{:S(2)}) copy-start(bf16[1,2048,128]{2,1,0:T(8,128)(2,1)} %param.11) | copy-start | bytes 1572868
  53.6 1.3 copy-start.1
  64.2 51.1 %copy-start.3 = (bf16[1,128,2048]{2,1,0:T(8,128)(2,1)S(1)}, bf16[1,128,2048]{2,1,0:T(8,128)(2,1)}, u32[]{:S(2)}) copy-start(bf16[1,128,2048]{2,1,0:T(8,128)(2,1)} %param.13) | copy-start | bytes 1572868
  64.2 77.8 %reduce-scatter.11.cloned.1.call-start = ((), (), s32[]{:S(2)}) async-start(), calls=%async_computation.7 | async-start | bytes 655360 | tf_op jit(solution)/shard_map/reduce_scatter | solution.py:93
  118.9 1.3 copy-start.5
  120.2 62.1 %reduce-scatter.13.cloned.1.call-start = ((), (), s32[]{:S(2)}) async-start(), calls=%async_computation.8 | async-start | bytes 294912
  143.8 3.2 %copy-start.2 = (f32[128,2176]{1,0:T(8,128)S(1)}, f32[128,2176]{1,0:T(8,128)}, u32[]{:S(2)}) copy-start(f32[128,2176]{1,0:T(8,128)} %reduce-scatter.7.cloned.1.call-done) | copy-start | bytes 3342340
  143.8 79.1 %reduce-scatter.9.cloned.1.call-start = ((), (), s32[]{:S(2)}) async-start(), calls=%async_computation.6 | async-start | bytes 1179648 | tf_op jit(solution)/shard_map/reduce_scatter | solution.py:77
Sparse Core Ops, SparseCore 0:
  64.3 50.9 reduce-scatter.6
  120.3 21.6 reduce-scatter.10
  144.5 37.7 reduce-scatter.12
  185.4 37.3 reduce-scatter.8
where the time goes:
time: 230 us; the launch traced here: 229 us
  waiting for transfers between devices  136 us (59%)
  blocking collectives  40.3 us (18%)
  matrix products  18.9 us (8%)
  local copies, waits for them, and re-layouts  14.6 us (6%)
  between operations  13.9 us (6%)
  other arithmetic  5.7 us (2%)
    reduce_scatter x1, waiting for transfers between devices, shards(): lax.psum_scatter(jnp.concatenate([keyval, ranks], axis=1), 'tensor', scat...  51 us
    reduce_scatter x1, waiting for transfers between devices, shards(): lax.psum_scatter(grad_a_term, 'dp', scatter_dimension=0, tiled=True)  39.1 us
    all_to_all x1, blocking collectives, shards(): lax.all_to_all(chosen.reshape(trials * tensors, select, normed_input), ('...  34.8 us
    unnamed x5, waiting for transfers between devices  31.7 us
    reduce_scatter x1, waiting for transfers between devices, shards(): lax.psum_scatter(up_gradient_term, 'tensor', scatter_dimension=1, tiled=T...  14 us
    reshape x2, local copies, waits for them, and re-layouts, shards(): chosen.reshape(trials, select, tensors, normed_input).transpose(0, 2, 1, 3)  7.26 us
    dot_general x1, matrix products, shards(): keyval = jnp.dot(rows, keyvalue_weight, preferred_element_type=jnp.float32)  6.88 us
    all_gather x1, blocking collectives, shards(): every_rank = lax.all_gather(rank_gradient, 'tensor', axis=0, tiled=True)  5.45 us
  transfers between devices with their start and end apart: 4, of which 4 were waited for; matrix products, arithmetic and copies ran while one was open for 5% of the time, Pallas kernels for 0%

commit v1 on v0

--- a/solution.py
+++ b/solution.py
@@ -53,7 +53,12 @@
     rank_gradient = (
         adapter_scale * jnp.concatenate([key_gradient_full, value_gradient_full], axis=1)
     ).astype(jnp.bfloat16)
-    every_rank = lax.all_gather(rank_gradient, "tensor", axis=0, tiled=True)
+    every_rank = jnp.concatenate(
+        lax.all_to_all(
+            jnp.stack([rank_gradient for _ in range(lax.axis_size("tensor"))], 0), "tensor", 0, 0
+        ),
+        0,
+    )
     grad_a_term = lax.dot_general(
         every_rank, rows, (((0,), (0,)), ((), ())), preferred_element_type=jnp.float32
     )

time: 230 us -> 230 us (level)
  blocking collectives: 40.3 us -> 34.8 us
  starting transfers between devices: 0.16 us -> 3.49 us
    all_gather x1 -> x0, blocking collectives: 5.45 us -> none  [shards(): every_rank = lax.all_gather(rank_gradient, 'tensor', axis=0, tiled=True)]
    all_to_all x0 -> x1, starting transfers between devices: none -> 3.33 us  [shards(): lax.all_to_all(jnp.stack([rank_gradient for _ in range(lax.axis_size('ten...]
  transfers between devices with their start and end apart: 4 -> 5, of which waited for: 4 -> 4; matrix products, arithmetic and copies ran while one was open for 5% -> 6% of each run, Pallas kernels for 0% -> 0%
where the time goes in v1:
time: 230 us; the launch traced here: 229 us
  waiting for transfers between devices  137 us (60%)
  blocking collectives  34.8 us (15%)
  matrix products  19 us (8%)
  local copies, waits for them, and re-layouts  15.3 us (7%)
  between operations  14 us (6%)
  other arithmetic  5.7 us (2%)
  starting transfers between devices  3.49 us (2%)
    reduce_scatter x1, waiting for transfers between devices, shards(): lax.psum_scatter(jnp.concatenate([keyval, ranks], axis=1), 'tensor', scat...  51 us
    reduce_scatter x1, waiting for transfers between devices, shards(): lax.psum_scatter(grad_a_term, 'dp', scatter_dimension=0, tiled=True)  39.1 us
    all_to_all x1, blocking collectives, shards(): lax.all_to_all(chosen.reshape(trials * tensors, select, normed_input), ('...  34.8 us
    unnamed x5, waiting for transfers between devices  31.9 us
    reduce_scatter x1, waiting for transfers between devices, shards(): lax.psum_scatter(up_gradient_term, 'tensor', scatter_dimension=1, tiled=T...  15 us
    reshape x2, local copies, waits for them, and re-layouts, shards(): chosen.reshape(trials, select, tensors, normed_input).transpose(0, 2, 1, 3)  7.25 us
    dot_general x1, matrix products, shards(): keyval = jnp.dot(rows, keyvalue_weight, preferred_element_type=jnp.float32)  6.88 us
  transfers between devices with their start and end apart: 5, of which 4 were waited for; matrix products, arithmetic and copies ran while one was open for 6% of the time, Pallas kernels for 0%

profile of v1, /device:TPU:4, one launch (start us, length us, event | category | flops | bytes accessed | tf_op | source)
XLA Modules:
  0.0 229.4 jit_solution(10652704652752377426)
XLA Ops:
  7.2 0.9 constant_dynamic-slice_fusion
  8.2 0.6 copy-done
  8.8 0.8 multiply_reduce_fusion
  9.6 1.9 multiply_convert_fusion
  11.5 4.5 %reshape.41 = bf16[8,16,4,2048]{3,2,1,0:T(4,128)(2,1)} reshape(bf16[128,8192]{1,0:T(8,128)(2,1)} %multiply_convert_fusion) | data formatting | bytes 4194304 | tf_op jit(solution)/shard_map/reshape | solution.py:36
  16.0 2.8 %copy.17 = bf16[8,16,4,2048]{3,1,2,0:T(8,128)(2,1)S(1)} copy(bf16[8,16,4,2048]{3,2,1,0:T(4,128)(2,1)} %reshape.41) | data formatting | bytes 4194304 | tf_op jit(solution)/shard_map/reshape | solution.py:36
  18.8 34.8 %all_to_all.10 = bf16[32,16,2048]{2,1,0:T(8,128)(2,1)S(1)} all-to-all(bf16[32,16,2048]{2,1,0:T(8,128)(2,1)S(1)} %bitcast.29), channel_id=1, replica_groups=mesh['trial'=8,'dp'=8,'tensor'=4] {'trial','tensor'}, dimensions={0} | all-to-all | bytes 4194304 | tf_op jit(solution)/shard_map/all_to_all | solution.py:37
  53.6 0.7 fusion.2
  54.3 0.6 copy-done.1
  54.9 6.9 %fusion.25 = f32[512,2048]{1,0:T(8,128)S(1)} fusion(bf16[512,2048]{1,0:T(8,128)(2,1)S(1)} %bitcast.27, bf16[2048,2048]{1,0:T(8,128)(2,1)} %param.10), kind=kOutput, calls=%fused_computation.35 | convolution fusion | flops 4294967296 | bytes 14680064 | tf_op jit(solution)/shard_map/dot_general | solution.py:66
  61.8 2.4 %pad_maximum_fusion = f32[512,2176]{1,0:T(8,128)} fusion(f32[512,128]{1,0:T(8,128)S(1)} %fusion.2, f32[512,2048]{1,0:T(8,128)S(1)} %fusion.25), kind=kLoop, calls=%fused_computation | loop fusion | flops 1114112 | bytes 8912896 | tf_op jit(solution)/shard_map/concatenate | solution.py:69
  64.2 51.0 %reduce-scatter.7.cloned.1.call-done = f32[128,2176]{1,0:T(8,128)} async-done(((f32[512,2176]{1,0:T(8,128)}), f32[128,2176]{1,0:T(8,128)}) %reduce-scatter.7.cloned.1.call-update) | async-done | bytes 1114128 | tf_op jit(solution)/shard_map/reduce_scatter | solution.py:68
  115.3 1.2 fusion.8
  116.4 0.3 concatenate.22
  116.8 1.4 fusion.4
  118.2 0.3 concatenate.23
  118.5 0.3 fusion.1
  119.0 1.2 reshape.45
  120.2 1.2 fusion.10
  121.3 1.2 fusion.6
  122.5 0.1 copy.19
  122.6 0.7 stack.2
  123.3 3.3 %all-to-all-start.1 = ((bf16[4,128,128]{2,1,0:T(8,128)(2,1)}), bf16[4,128,128]{2,1,0:T(8,128)(2,1)S(1)}, u32[]{:S(2)}, u32[]{:S(2)}) async-start(bf16[4,128,128]{2,1,0:T(8,128)(2,1)} %stack.2), calls=%async_computation.2 | async-start | bytes 262144 | tf_op jit(solution)/shard_map/all_to_all | solution.py:57
  126.7 15.0 %reduce-scatter.11.cloned.1.call-done = f32[64,512]{1,0:T(8,128)} async-done(((f32[64,2048]{1,0:T(8,128)}), f32[64,512]{1,0:T(8,128)}) %reduce-scatter.11.cloned.1.call-update) | async-done | bytes 131088 | tf_op jit(solution)/shard_map/reduce_scatter | solution.py:98
  141.7 1.7 copy.22
  143.5 3.1 %fusion.26 = f32[128,2048]{1,0:T(8,128)} fusion(bf16[512,128]{1,0:T(8,128)(2,1)S(1)} %bitcast.31, bf16[512,2048]{1,0:T(8,128)(2,1)} %bitcast.28), kind=kOutput, calls=%fused_computation.36 | convolution fusion | flops 268435456 | bytes 3276800 | tf_op jit(solution)/shard_map/dot_general | solution.py:62
  146.7 1.3 fusion.13
  148.0 1.3 fusion.16
  149.3 1.1 fusion
  150.4 31.9 %reduce-scatter.13.cloned.1.call-done = f32[64,64]{1,0:T(8,128)} async-done(((f32[512,64]{1,0:T(8,128)}), f32[64,64]{1,0:T(8,128)}) %reduce-scatter.13.cloned.1.call-update) | async-done | bytes 16400
  182.3 1.5 copy.23
  183.7 39.1 %reduce-scatter.9.cloned.1.call-done = f32[16,2048]{1,0:T(8,128)} async-done(((f32[128,2048]{1,0:T(8,128)}), f32[16,2048]{1,0:T(8,128)}) %reduce-scatter.9.cloned.1.call-update) | async-done | bytes 131088 | tf_op jit(solution)/shard_map/reduce_scatter | solution.py:82
  (25 shorter events, 0.4 us)
Async XLA Ops:
  7.2 1.6 copy-start
  7.2 108.1 %reduce-scatter.7.cloned.1.call-start = ((), (), s32[]{:S(2)}) async-start(), calls=%async_computation.6 | async-start | bytes 5570560 | tf_op jit(solution)/shard_map/reduce_scatter | solution.py:68
  8.8 0.8 copy-start.6
  18.7 34.8 %copy-start.4 = (bf16[1,2048,128]{2,1,0:T(8,128)(2,1)S(1)}, bf16[1,2048,128]{2,1,0:T(8,128)(2,1)}, u32[]{:S(2)}) copy-start(bf16[1,2048,128]{2,1,0:T(8,128)(2,1)} %param.11) | copy-start | bytes 1572868
  53.6 1.3 copy-start.1
  64.2 51.1 %copy-start.3 = (bf16[1,128,2048]{2,1,0:T(8,128)(2,1)S(1)}, bf16[1,128,2048]{2,1,0:T(8,128)(2,1)}, u32[]{:S(2)}) copy-start(bf16[1,128,2048]{2,1,0:T(8,128)(2,1)} %param.13) | copy-start | bytes 1572868
  64.2 77.5 %reduce-scatter.11.cloned.1.call-start = ((), (), s32[]{:S(2)}) async-start(), calls=%async_computation.8 | async-start | bytes 655360 | tf_op jit(solution)/shard_map/reduce_scatter | solution.py:98
  118.9 1.3 copy-start.5
  123.3 20.2 %all-to-all-start.1 = ((bf16[4,128,128]{2,1,0:T(8,128)(2,1)}), bf16[4,128,128]{2,1,0:T(8,128)(2,1)S(1)}, u32[]{:S(2)}, u32[]{:S(2)}) async-start(bf16[4,128,128]{2,1,0:T(8,128)(2,1)} %stack.2), calls=%async_computation.2 | async-start | bytes 262144 | tf_op jit(solution)/shard_map/all_to_all | solution.py:57
  126.6 55.7 %reduce-scatter.13.cloned.1.call-start = ((), (), s32[]{:S(2)}) async-start(), calls=%async_computation.9 | async-start | bytes 294912
  143.5 79.4 %reduce-scatter.9.cloned.1.call-start = ((), (), s32[]{:S(2)}) async-start(), calls=%async_computation.7 | async-start | bytes 1179648 | tf_op jit(solution)/shard_map/reduce_scatter | solution.py:82
  143.5 3.2 %copy-start.2 = (f32[128,2176]{1,0:T(8,128)S(1)}, f32[128,2176]{1,0:T(8,128)}, u32[]{:S(2)}) copy-start(f32[128,2176]{1,0:T(8,128)} %reduce-scatter.7.cloned.1.call-done) | copy-start | bytes 3342340
Sparse Core Ops, SparseCore 0:
  64.3 50.9 reduce-scatter.6
  120.3 21.3 reduce-scatter.10
  144.2 38.0 reduce-scatter.12
  185.4 37.4 reduce-scatter.8
